TPU v7x, 32 devices: a whole 2x2x4 slice. The times are simulated.
32 devices in a mesh: seq: 4 (over y, x), res: 8 (over z, core).
Axes of the slice: x: 2, y: 2, z: 4, core: 2. Of those that a mesh axis runs over, the one named last changes fastest.
Arguments:
- alignment: float32 [256, 64, 256], P('seq', 'res'), may hold values from -100 to 100
- pair_features: float32 [64, 64, 128], P('seq', 'res'), may hold values from -100 to 100
- outer_gain: float32 [256], replicated, may hold values from 0.5 to 1.5
- w_outer_in: float32 [256, 64], replicated, may hold values from -0.375 to 0.375
- w_outer_out: float32 [1024, 128], replicated, may hold values from -0.1875 to 0.1875
- pair_gain: float32 [128], replicated, may hold values from 0.5 to 1.5
- w_bias: float32 [128, 8], replicated, may hold values from -30 to 30
- row_gain: float32 [256], replicated, may hold values from 0.5 to 1.5
- w_project: float32 [256, 1024], replicated, may hold values from -0.375 to 0.375
- w_output: float32 [256, 256], replicated, may hold values from -0.375 to 0.375
Outputs:
- alignment_out: float32 [256, 64, 256], P('seq', 'res')
- updated_pair_array: float32 [64, 64, 128], P('seq', 'res')
All inputs are finite; a program needn't handle non-finite values.
Results may differ from a plain program's by a relative error of at most 0.00018.
Values sent between devices are 32-bit elements; how exact they have to be, the bound alone decides.
A program may use at most 128 MiB of HBM per device.

v0:
```python
import jax
import jax.numpy as jnp
from jax import lax
from jax.sharding import PartitionSpec as P

precise = lax.Precision.HIGHEST


def layer_norm(values, scales):
    average = jnp.mean(values, axis=-1, keepdims=True)
    centered = values - average
    variance = jnp.mean(centered * centered, axis=-1, keepdims=True)
    return centered * lax.rsqrt(variance + 1e-05) * scales


def row_attention(sequence, bias_all, row_gain, w_project, w_output):
    residues, channels = sequence.shape
    head_count = bias_all.shape[0]
    head_size = channels // head_count
    normed_rows = layer_norm(sequence, row_gain)
    projected = jnp.dot(
        normed_rows, w_project, precision=precise, preferred_element_type=jnp.float32
    )
    query_map = projected[:, :channels].reshape(residues, head_count, head_size) * head_size ** (
        -0.5
    )
    key_map = projected[:, channels : 2 * channels].reshape(residues, head_count, head_size)
    value_map = projected[:, 2 * channels : 3 * channels].reshape(residues, head_count, head_size)
    gate_map = projected[:, 3 * channels :]
    scores = jnp.einsum("ihd,jhd->hij", query_map, key_map, precision=precise) + bias_all
    weights = jax.nn.softmax(scores, axis=-1)
    mixed_heads = jnp.einsum("hij,jhd->ihd", weights, value_map, precision=precise).reshape(
        residues, channels
    )
    gated_out = jax.nn.sigmoid(gate_map) * mixed_heads
    return sequence + jnp.dot(
        gated_out, w_output, precision=precise, preferred_element_type=jnp.float32
    )


def on_device(
    alignment,
    pair_features,
    outer_gain,
    w_outer_in,
    w_outer_out,
    pair_gain,
    w_bias,
    row_gain,
    w_project,
    w_output,
):
    sequence_local_count, residue_local_count, alignment_channel_count = alignment.shape
    row_block = pair_features.shape[0]
    sequence_group_list = lax.axis_size("res")
    seq_groups = lax.axis_size("seq")
    seq_total = sequence_local_count * seq_groups
    channels = w_outer_in.shape[1] // 2
    normed_rows = layer_norm(alignment, outer_gain)
    both_maps = jnp.einsum("src,cd->sdr", normed_rows, w_outer_in, precision=precise)
    left_maps = both_maps[:, :channels]
    right_maps = both_maps[:, channels:]
    left_all = lax.all_gather(left_maps, "res", axis=2, tiled=True)
    left_rows = lax.all_to_all(left_all, "seq", split_axis=2, concat_axis=0, tiled=True)
    product = jnp.einsum(
        "sxi,syj->ijxy",
        left_rows,
        lax.all_gather(right_maps, "seq", axis=0, tiled=True),
        precision=precise,
    )
    summed = product.reshape(row_block, residue_local_count, channels * channels)
    pair_update = jnp.einsum("ijk,kc->ijc", summed / seq_total, w_outer_out, precision=precise)
    updated_pair_array = pair_features + pair_update
    bias_tile = jnp.einsum(
        "ijc,ch->hij", layer_norm(updated_pair_array, pair_gain), w_bias, precision=precise
    )
    bias_rows = lax.all_gather(bias_tile, "res", axis=2, tiled=True)
    bias_all = lax.all_gather(bias_rows, "seq", axis=1, tiled=True)
    sequence_grouped_rows = alignment.reshape(
        sequence_group_list,
        sequence_local_count // sequence_group_list,
        residue_local_count,
        alignment_channel_count,
    )
    sequences = lax.all_to_all(
        sequence_grouped_rows, "res", split_axis=0, concat_axis=2, tiled=True
    )[0]
    updated = jax.vmap(row_attention, in_axes=(0, None, None, None, None))(
        sequences, bias_all, row_gain, w_project, w_output
    )
    attended = updated[None]
    returned_result = lax.all_to_all(attended, "res", split_axis=2, concat_axis=0, tiled=True)
    return (
        returned_result.reshape(sequence_local_count, residue_local_count, alignment_channel_count),
        updated_pair_array,
    )


def solution(mesh):
    in_specs = (
        P("seq", "res", None),
        P("seq", "res", None),
        P(),
        P(),
        P(),
        P(),
        P(),
        P(),
        P(),
        P(),
    )
    out_specs = (P("seq", "res", None), P("seq", "res", None))
    return jax.shard_map(
        on_device, mesh=mesh, in_specs=in_specs, out_specs=out_specs, check_vma=False
    )
```

profile of v0, /device:TPU:0, one launch (start us, length us, event | category | flops | bytes accessed | tf_op | source)
XLA Modules:
  0.0 148.9 jit_solution(3641051938862273192)
XLA Ops:
  0.6 1.3 reduce_sum.65
  1.9 1.3 multiply_reduce_fusion
  3.2 1.7 %convolution_bitcast_fusion = f32[64,64,8]{1,2,0:T(8,128)S(1)} fusion(f32[64,8,256]{2,1,0:T(8,128)} %param.10, f32[256]{0:T(256)} %param.12, f32[64,8]{1,0:T(8,128)S(1)} %add_rsqrt_fusion, f32[64,8]{1,0:T(8,128)S(1)} %broadcast_multiply_fusion, f32[256,64]{0,1:T(8,128)} %param.13), kind=kOutput, calls=%fused_computation.8 | convolution fusion | flops 101056512 | bytes 726016 | tf_op jit(solution)/shard_map/src,cd->sdr/dot_general | solution.py:60
  5.1 25.1 %all_gather.13 = f32[64,32,64]{1,2,0:T(8,128)S(1)} all-gather(f32[64,32,8]{1,2,0:T(8,128)S(1)} %get-tuple-element.5), channel_id=1, replica_groups=mesh['seq'=4,'res'=8] {'res'}, dimensions={2}, use_global_device_ids=true | all-gather | bytes 589824 | tf_op jit(solution)/shard_map/all_gather | solution.py:63
  30.2 2.1 %copy.39 = f32[64,32,64]{0,1,2:T(8,128)} copy(f32[64,32,64]{1,2,0:T(8,128)S(1)} %all_gather.13) | data formatting | bytes 1048576 | tf_op jit(solution)/shard_map/all_gather | solution.py:63
  32.3 2.7 %reshape.99 = f32[4,1,32768]{2,1,0:T(1,128)} reshape(f32[64,32,64]{2,1,0:T(8,128)} %bitcast.73) | data formatting | bytes 1048576
  35.0 3.7 %all-to-all-start.1 = ((f32[4,1,32768]{2,1,0:T(1,128)}), f32[4,1,32768]{2,1,0:T(1,128)S(1)}, u32[]{:S(2)}, u32[]{:S(2)}) async-start(f32[4,1,32768]{2,1,0:T(1,128)} %reshape.99), calls=%async_computation.1 | async-start | bytes 1048576 | tf_op jit(solution)/shard_map/all_to_all | solution.py:64
  38.7 18.5 %all_gather.12 = f32[256,32,8]{1,2,0:T(8,128)S(1)} all-gather(f32[64,32,8]{1,2,0:T(8,128)S(1)} %get-tuple-element.6), channel_id=1, replica_groups=mesh['seq'=4,'res'=8] {'seq'}, dimensions={0}, use_global_device_ids=true | all-gather | bytes 327680 | tf_op jit(solution)/shard_map/all_gather | solution.py:68
  57.6 4.3 %all-to-all-start = ((f32[8,8,8,256]{3,2,1,0:T(8,128)}), f32[8,8,8,256]{3,2,1,0:T(8,128)}, u32[]{:S(2)}, u32[]{:S(2)}) async-start(f32[8,8,8,256]{3,2,1,0:T(8,128)} %bitcast), calls=%async_computation | async-start | bytes 1048576 | tf_op jit(solution)/shard_map/all_to_all | solution.py:85
  62.5 2.1 %reduce.2 = f32[4,32768]{1,0:T(4,128)S(1)} reduce(f32[4,1,32768]{2,1,0:T(1,128)S(1)} %all-to-all-done.1, f32[]{:T(128)} %broadcast.97), dimensions={1}, to_apply=%all_to_all.38.reduce_sub_computation | reduce | bytes 1048580 | tf_op jit(solution)/shard_map/all_to_all | solution.py:64
  65.2 0.7 copy.59
  65.9 0.6 reshape.94
  66.5 3.2 %multiply_bitcast_fusion = f32[16,8,32,32]{2,1,0,3:T(8,128)} fusion(f32[256,32,8,1]{0,2,3,1:T(8,128)S(1)} %copy.49, f32[256,32,16,1]{0,1,2,3:T(8,128)S(1)} %reshape.94), kind=kOutput, calls=%fused_computation.3 | convolution fusion | flops 402784256 | bytes 1310720 | tf_op jit(solution)/shard_map/sxi,syj->ijxy/dot_general | solution.py:65
  69.7 2.3 %copy.42 = f32[16,8,32,32]{3,2,1,0:T(8,128)S(1)} copy(f32[16,8,32,32]{2,1,0,3:T(8,128)} %multiply_bitcast_fusion) | data formatting | bytes 1048576 | tf_op jit(solution)/shard_map/div | solution.py:72
  72.0 1.7 %div.50 = f32[16,8,1024]{2,1,0:T(8,128)} reshape(f32[16,8,32,32]{3,2,1,0:T(8,128)S(1)} %copy.42) | data formatting | bytes 1048576 | tf_op jit(solution)/shard_map/div | solution.py:72
  73.7 1.9 %fusion.41 = (f32[16,8]{1,0:T(8,128)S(1)}, f32[16,8,128]{2,1,0:T(8,128)S(1)}) fusion(f32[16,8,128]{2,1,0:T(8,128)S(1)} %copy-done.3, f32[16,8,1024]{2,1,0:T(8,128)} %div.50, f32[1024,128]{1,0:T(8,128)} %param.14), kind=kOutput, calls=%fused_computation.60 | convolution fusion | flops 201359232 | bytes 1180160 | tf_op jit(solution)/shard_map/ijk,kc->ijc/dot_general | solution.py:72
  76.1 14.9 %all_gather.14 = f32[8,16,64]{0,2,1:T(8,128)S(1)} all-gather(f32[8,16,8]{0,2,1:T(8,128)S(1)} %convolution_bitcast_fusion.1), channel_id=1, replica_groups=mesh['seq'=4,'res'=8] {'res'}, dimensions={2}, use_global_device_ids=true | all-gather | bytes 36864 | tf_op jit(solution)/shard_map/all_gather | solution.py:77
  91.2 8.4 %all_gather.15 = f32[8,64,64]{2,0,1:T(8,128)S(1)} all-gather(f32[8,16,64]{2,0,1:T(8,128)S(1)} %copy.43), channel_id=1, replica_groups=mesh['seq'=4,'res'=8] {'seq'}, dimensions={1}, use_global_device_ids=true | all-gather | bytes 163840 | tf_op jit(solution)/shard_map/all_gather | solution.py:78
  99.8 1.2 bitcast_reduce_fusion
  101.1 1.3 multiply_reduce_fusion.1
  102.5 2.9 %fusion.4 = f32[8,64,1024]{2,1,0:T(8,128)S(1)} fusion(f32[256,1024]{1,0:T(8,128)S(1)} %copy-done, f32[256]{0:T(256)S(1)} %copy-done.4, f32[8,64]{1,0:T(8,128)S(1)} %rsqrt.28, f32[8,64]{1,0:T(8,128)S(1)} %div.42, f32[8,8,8,256]{3,2,1,0:T(8,128)} %all-to-all-done), kind=kOutput, calls=%fused_computation.11 | convolution fusion | flops 1611005952 | bytes 3675136 | tf_op jit(solution)/shard_map/vmap()/dot_general | solution.py:21
  105.5 1.2 fusion.39
  106.7 2.4 %copy.38 = f32[8,64,256]{1,2,0:T(8,128)} copy(f32[8,64,256]{2,1,0:T(8,128)} %get-tuple-element.2) | data formatting | bytes 1048576 | tf_op jit(solution)/shard_map/vmap()/slice | solution.py:27
  109.1 2.4 %copy.37 = f32[8,64,256]{1,2,0:T(8,128)} copy(f32[8,64,256]{2,1,0:T(8,128)} %get-tuple-element.3) | data formatting | bytes 1048576 | tf_op jit(solution)/shard_map/vmap()/mul | solution.py:24
  111.5 2.4 %copy.36 = f32[8,64,256]{1,2,0:T(8,128)} copy(f32[8,64,256]{2,1,0:T(8,128)} %get-tuple-element.4) | data formatting | bytes 1048576 | tf_op jit(solution)/shard_map/vmap()/slice | solution.py:28
  113.8 5.1 %add_reduce_fusion = (f32[8,8,64]{2,1,0:T(8,128)S(1)}, f32[8,8,64,64]{2,3,1,0:T(8,128)S(1)}) fusion(f32[8,64,64]{1,2,0:T(8,128)S(1)} %copy.44, f32[8,64,8,32]{1,3,2,0:T(8,128)} %bitcast.72, f32[8,64,8,32]{1,3,2,0:T(8,128)} %bitcast.71), kind=kOutput, calls=%fused_computation.4 | convolution fusion | flops 101183488 | bytes 2244608 | tf_op jit(solution)/shard_map/vmap(ihd,jhd->hij)/dot_general | solution.py:30
  119.5 0.7 copy-done.1
  120.2 3.3 %fusion = f32[8,8,32,64]{3,2,1,0:T(8,128)} fusion(f32[8,64,8,32]{1,3,2,0:T(8,128)S(1)} %bitcast.78, f32[8,8,64,64]{2,3,1,0:T(8,128)S(1)} %get-tuple-element.10, f32[8,8,64]{2,1,0:T(8,128)S(1)} %fusion.2, f32[8,8,64]{2,1,0:T(8,128)S(1)} %get-tuple-element.9, f32[8,64,64]{1,2,0:T(8,128)S(1)} %copy.44), kind=kOutput, calls=%fused_computation | convolution fusion | flops 101449728 | bytes 2260992 | tf_op jit(solution)/shard_map/vmap(hij,jhd->ihd)/dot_general | solution.py:32
  123.5 2.3 %copy.46 = f32[8,64,256]{2,1,0:T(8,128)} copy(f32[8,64,256]{1,2,0:T(8,128)} %bitcast.79) | data formatting | bytes 1048576 | tf_op jit(solution)/shard_map/vmap()/reshape | solution.py:32
  125.8 1.9 %fusion.3 = f32[1,8,64,256]{3,2,1,0:T(8,128)S(1)} fusion(f32[8,64,256]{2,1,0:T(8,128)} %copy.46, f32[8,64,1024]{2,1,0:T(8,128)S(1)} %fusion.4, f32[256,256]{1,0:T(8,128)} %param.19, f32[8,8,8,256]{3,2,1,0:T(8,128)} %all-to-all-done), kind=kOutput, calls=%fused_computation.7 | convolution fusion | flops 403308544 | bytes 2359296 | tf_op jit(solution)/shard_map/vmap()/dot_general | solution.py:36
  128.1 19.8 %all_to_all.48 = f32[1,8,64,256]{3,1,0,2:T(8,128)S(1)} all-to-all(f32[1,8,64,256]{3,1,0,2:T(8,128)S(1)} %copy.47), channel_id=1, replica_groups=mesh['seq'=4,'res'=8] {'res'}, dimensions={2} | all-to-all | bytes 1048576 | tf_op jit(solution)/shard_map/all_to_all | solution.py:92
  148.0 1.0 copy.48
  (35 shorter events, 3.4 us)
Async XLA Ops:
  0.6 101.9 %copy-start = (f32[256,1024]{1,0:T(8,128)S(1)}, f32[256,1024]{1,0:T(8,128)}, u32[]{:S(2)}) copy-start(f32[256,1024]{1,0:T(8,128)} %param.18) | copy-start | bytes 3145732
  35.0 22.6 %all-to-all-start.1 = ((f32[4,1,32768]{2,1,0:T(1,128)}), f32[4,1,32768]{2,1,0:T(1,128)S(1)}, u32[]{:S(2)}, u32[]{:S(2)}) async-start(f32[4,1,32768]{2,1,0:T(1,128)} %reshape.99), calls=%async_computation.1 | async-start | bytes 1048576 | tf_op jit(solution)/shard_map/all_to_all | solution.py:64
  57.6 42.2 %all-to-all-start = ((f32[8,8,8,256]{3,2,1,0:T(8,128)}), f32[8,8,8,256]{3,2,1,0:T(8,128)}, u32[]{:S(2)}, u32[]{:S(2)}) async-start(f32[8,8,8,256]{3,2,1,0:T(8,128)} %bitcast), calls=%async_computation | async-start | bytes 1048576 | tf_op jit(solution)/shard_map/all_to_all | solution.py:85
  71.9 1.8 %copy-start.3 = (f32[16,8,128]{2,1,0:T(8,128)S(1)}, f32[16,8,128]{2,1,0:T(8,128)}, u32[]{:S(2)}) copy-start(f32[16,8,128]{2,1,0:T(8,128)} %param.11) | copy-start | bytes 196612
  71.9 3.9 %copy-start.5 = (f32[128,8]{0,1:T(8,128)S(1)}, f32[128,8]{0,1:T(8,128)}, u32[]{:S(2)}) copy-start(f32[128,8]{0,1:T(8,128)} %param.16) | copy-start | bytes 12292
  71.9 3.9 %copy-start.6 = (f32[128]{0:T(128)S(1)}, f32[128]{0:T(128)}, u32[]{:S(2)}) copy-start(f32[128]{0:T(128)} %param.15) | copy-start | bytes 1540
  75.6 29.8 %copy-start.2 = (f32[16,8,128]{2,1,0:T(8,128)}, f32[16,8,128]{2,1,0:T(8,128)S(1)}, u32[]{:S(2)}) copy-start(f32[16,8,128]{2,1,0:T(8,128)S(1)} %get-tuple-element.8) | copy-start | bytes 196612
  75.6 26.9 %copy-start.4 = (f32[256]{0:T(256)S(1)}, f32[256]{0:T(256)}, u32[]{:S(2)}) copy-start(f32[256]{0:T(256)} %param.17) | copy-start | bytes 3076
  118.9 1.2 copy-start.1
where the time goes:
time: 150 us; the launch traced here: 149 us
  blocking collectives  86.8 us (58%)
  local copies, waits for them, and re-layouts  23.6 us (16%)
  matrix products  20.3 us (14%)
  other arithmetic  9.14 us (6%)
  starting transfers between devices  8.05 us (5%)
    all_gather x1, blocking collectives, on_device(): left_all = lax.all_gather(left_maps, 'res', axis=2, tiled=True)  25.1 us
    all_to_all x1, blocking collectives, on_device(): lax.all_to_all(attended, 'res', split_axis=2, concat_axis=0, tiled=True)  19.8 us
    all_gather x1, blocking collectives, on_device(): lax.all_gather(right_maps, 'seq', axis=0, tiled=True)  18.5 us
    all_gather x1, blocking collectives, on_device(): bias_rows = lax.all_gather(bias_tile, 'res', axis=2, tiled=True)  14.9 us
    all_gather x1, blocking collectives, on_device(): bias_all = lax.all_gather(bias_rows, 'seq', axis=1, tiled=True)  8.4 us
    dot_general x1, matrix products, row_attention(): jnp.einsum('ihd,jhd->hij', query_map, key_map, precision=precise) + bias_all  5.09 us
    all_to_all x1, starting transfers between devices, on_device(): lax.all_to_all(sequence_grouped_rows, 'res', split_axis=0, concat_axis=2,...  4.34 us
    div x2, local copies, waits for them, and re-layouts, on_device(): summed / seq_total  4 us
  transfers between devices with their start and end apart: 2, of which 0 were waited for; matrix products, arithmetic and copies ran while one was open for 10% of the time, Pallas kernels for 0%

commit v1 on v0

--- a/solution.py
+++ b/solution.py
@@ -4,6 +4,11 @@
 from jax.sharding import PartitionSpec as P
 
 precise = lax.Precision.HIGHEST
+
+
+def exchange_gather(array, axis, along):
+    stack = jnp.stack([array] * lax.axis_size(axis))
+    return jnp.concatenate(lax.all_to_all(stack, axis, 0, 0), axis=along)
 
 
 def layer_norm(values, scales):
@@ -63,10 +68,7 @@
     left_all = lax.all_gather(left_maps, "res", axis=2, tiled=True)
     left_rows = lax.all_to_all(left_all, "seq", split_axis=2, concat_axis=0, tiled=True)
     product = jnp.einsum(
-        "sxi,syj->ijxy",
-        left_rows,
-        lax.all_gather(right_maps, "seq", axis=0, tiled=True),
-        precision=precise,
+        "sxi,syj->ijxy", left_rows, exchange_gather(right_maps, "seq", 0), precision=precise
     )
     summed = product.reshape(row_block, residue_local_count, channels * channels)
     pair_update = jnp.einsum("ijk,kc->ijc", summed / seq_total, w_outer_out, precision=precise)

time: 150 us -> 147 us (0.980)
  blocking collectives: 86.8 us -> 67.8 us
  starting transfers between devices: 8.05 us -> 13.7 us
  waiting for transfers between devices: 0.01 us -> 5.55 us
  local copies, waits for them, and re-layouts: 23.6 us -> 26.3 us
    all_gather x1 -> x0, blocking collectives: 18.5 us -> none  [on_device(): lax.all_gather(right_maps, 'seq', axis=0, tiled=True)]
    all_to_all x1, waiting for transfers between devices: 0.01 us -> 5.54 us  [on_device(): lax.all_to_all(left_all, 'seq', split_axis=2, concat_axis=0, tiled=True)]
    all_to_all x0 -> x1, starting transfers between devices: none -> 5.19 us  [exchange_gather(): return jnp.concatenate(lax.all_to_all(stack, axis, 0, 0), axis=along)]
    unnamed x16 -> x21, local copies, waits for them, and re-layouts: 3.91 us -> 7.14 us
    dot_general x1, matrix products: 3.15 us -> 4.83 us  [on_device(): jnp.einsum('sxi,syj->ijxy', left_rows, exchange_gather(right_maps, 'seq',...]
  transfers between devices with their start and end apart: 2 -> 3, of which waited for: 0 -> 1; matrix products, arithmetic and copies ran while one was open for 10% -> 15% of each run, Pallas kernels for 0% -> 0%
where the time goes in v1:
time: 147 us; the launch traced here: 146 us
  blocking collectives  67.8 us (46%)
  local copies, waits for them, and re-layouts  26.3 us (18%)
  matrix products  20.8 us (14%)
  starting transfers between devices  13.7 us (9%)
  other arithmetic  10.5 us (7%)
  waiting for transfers between devices  5.55 us (4%)
    all_gather x1, blocking collectives, on_device(): left_all = lax.all_gather(left_maps, 'res', axis=2, tiled=True)  23.9 us
    all_to_all x1, blocking collectives, on_device(): lax.all_to_all(attended, 'res', split_axis=2, concat_axis=0, tiled=True)  19.8 us
    all_gather x1, blocking collectives, on_device(): bias_rows = lax.all_gather(bias_tile, 'res', axis=2, tiled=True)  14.9 us
    all_gather x1, blocking collectives, on_device(): bias_all = lax.all_gather(bias_rows, 'seq', axis=1, tiled=True)  9.15 us
    unnamed x21, local copies, waits for them, and re-layouts  7.14 us
    all_to_all x1, waiting for transfers between devices, on_device(): lax.all_to_all(left_all, 'seq', split_axis=2, concat_axis=0, tiled=True)  5.54 us
    all_to_all x1, starting transfers between devices, exchange_gather(): return jnp.concatenate(lax.all_to_all(stack, axis, 0, 0), axis=along)  5.19 us
    dot_general x1, matrix products, row_attention(): jnp.einsum('ihd,jhd->hij', query_map, key_map, precision=precise) + bias_all  5.09 us
  transfers between devices with their start and end apart: 3, of which 1 were waited for; matrix products, arithmetic and copies ran while one was open for 15% of the time, Pallas kernels for 0%

profile of v1, /device:TPU:0, one launch (start us, length us, event | category | flops | bytes accessed | tf_op | source)
XLA Modules:
  0.0 145.6 jit_solution(1293706428506713598)
XLA Ops:
  0.6 1.3 reduce_sum.65
  1.9 1.3 multiply_reduce_fusion
  3.2 1.7 %convolution_bitcast_fusion = f32[64,64,8]{1,2,0:T(8,128)S(1)} fusion(f32[64,8,256]{2,1,0:T(8,128)} %param.10, f32[256]{0:T(256)} %param.12, f32[64,8]{1,0:T(8,128)S(1)} %add_rsqrt_fusion, f32[64,8]{1,0:T(8,128)S(1)} %broadcast_multiply_fusion, f32[256,64]{0,1:T(8,128)} %param.13), kind=kOutput, calls=%fused_computation.9 | convolution fusion | flops 101056512 | bytes 726016 | tf_op jit(solution)/shard_map/src,cd->sdr/dot_general | solution.py:65
  5.9 1.0 reshape.104
  7.0 5.2 %all-to-all-start.1 = ((f32[4,1,16384]{2,1,0:T(1,128)}), f32[4,1,16384]{2,1,0:T(1,128)S(1)}, u32[]{:S(2)}, u32[]{:S(2)}) async-start(f32[4,1,16384]{2,1,0:T(1,128)} %reshape.104), calls=%async_computation.1 | async-start | bytes 524288 | tf_op jit(solution)/shard_map/all_to_all | solution.py:11
  12.1 23.9 %all_gather.9 = f32[64,32,64]{1,2,0:T(8,128)S(1)} all-gather(f32[64,32,8]{1,2,0:T(8,128)} %get-tuple-element.6), channel_id=1, replica_groups=mesh['seq'=4,'res'=8] {'res'}, dimensions={2}, use_global_device_ids=true | all-gather | bytes 589824 | tf_op jit(solution)/shard_map/all_gather | solution.py:68
  36.0 2.1 %copy.56 = f32[64,32,64]{0,1,2:T(8,128)} copy(f32[64,32,64]{1,2,0:T(8,128)S(1)} %all_gather.9) | data formatting | bytes 1048576 | tf_op jit(solution)/shard_map/all_gather | solution.py:68
  38.1 2.7 %reshape.102 = f32[4,1,32768]{2,1,0:T(1,128)} reshape(f32[64,32,64]{2,1,0:T(8,128)} %bitcast.86) | data formatting | bytes 1048576
  40.8 4.2 %all-to-all-start.2 = ((f32[4,1,32768]{2,1,0:T(1,128)}), f32[4,1,32768]{2,1,0:T(1,128)S(1)}, u32[]{:S(2)}, u32[]{:S(2)}) async-start(f32[4,1,32768]{2,1,0:T(1,128)} %reshape.102), calls=%async_computation.2 | async-start | bytes 1048576 | tf_op jit(solution)/shard_map/all_to_all | solution.py:69
  45.5 1.4 reduce.3
  46.9 1.1 reshape.105
  48.0 5.5 %all-to-all-done.2 = f32[4,1,32768]{2,1,0:T(1,128)S(1)} async-done(((f32[4,1,32768]{2,1,0:T(1,128)}), f32[4,1,32768]{2,1,0:T(1,128)S(1)}, u32[]{:S(2)}, u32[]{:S(2)}) %all-to-all-start.2) | async-done | bytes 524320 | tf_op jit(solution)/shard_map/all_to_all | solution.py:69
  53.5 4.3 %all-to-all-start = ((f32[8,8,8,256]{3,2,1,0:T(8,128)}), f32[8,8,8,256]{3,2,1,0:T(8,128)}, u32[]{:S(2)}, u32[]{:S(2)}) async-start(f32[8,8,8,256]{3,2,1,0:T(8,128)} %bitcast), calls=%async_computation | async-start | bytes 1048576 | tf_op jit(solution)/shard_map/all_to_all | solution.py:87
  57.9 2.1 %reduce.2 = f32[4,32768]{1,0:T(4,128)S(1)} reduce(f32[4,1,32768]{2,1,0:T(1,128)S(1)} %all-to-all-done.2, f32[]{:T(128)} %broadcast.99), dimensions={1}, to_apply=%all_to_all.40.reduce_sub_computation | reduce | bytes 1048580 | tf_op jit(solution)/shard_map/all_to_all | solution.py:69
  60.0 1.5 %reshape.103 = f32[64,32,64]{2,1,0:T(8,128)} reshape(f32[4,32768]{1,0:T(4,128)S(1)} %reduce.2) | data formatting | bytes 1048576
  61.5 4.8 %fusion = f32[16,8,32,32]{2,3,0,1:T(8,128)S(1)} fusion(f32[64,32,4,16]{0,1,3,2:T(8,128)} %bitcast.85, f32[4,8,32,64]{3,2,1,0:T(8,128)} %reshape.105), kind=kOutput, calls=%fused_computation.1 | convolution fusion | flops 402784256 | bytes 1310720 | tf_op jit(solution)/shard_map/sxi,syj->ijxy/dot_general | solution.py:70
  66.4 1.9 %copy.60 = f32[16,8,32,32]{3,2,1,0:T(8,128)} copy(f32[16,8,32,32]{2,3,0,1:T(8,128)S(1)} %fusion) | data formatting | bytes 1048576 | tf_op jit(solution)/shard_map/div | solution.py:74
  68.3 2.5 %div.50 = f32[16,8,1024]{2,1,0:T(8,128)S(1)} reshape(f32[16,8,32,32]{3,2,1,0:T(8,128)} %copy.60) | data formatting | bytes 1048576 | tf_op jit(solution)/shard_map/div | solution.py:74
  72.0 14.9 %all_gather.10 = f32[8,16,64]{0,2,1:T(8,128)S(1)} all-gather(f32[8,16,8]{0,2,1:T(8,128)S(1)} %convolution_bitcast_fusion.1), channel_id=1, replica_groups=mesh['seq'=4,'res'=8] {'res'}, dimensions={2}, use_global_device_ids=true | all-gather | bytes 36864 | tf_op jit(solution)/shard_map/all_gather | solution.py:79
  87.1 9.2 %all_gather.11 = f32[8,64,64]{2,0,1:T(8,128)S(1)} all-gather(f32[8,16,64]{2,0,1:T(8,128)S(1)} %copy.61), channel_id=1, replica_groups=mesh['seq'=4,'res'=8] {'seq'}, dimensions={1}, use_global_device_ids=true | all-gather | bytes 163840 | tf_op jit(solution)/shard_map/all_gather | solution.py:80
  96.4 1.2 bitcast_reduce_fusion
  97.7 1.3 multiply_reduce_fusion.1
  99.2 2.9 %fusion.7 = f32[8,64,1024]{2,1,0:T(8,128)S(1)} fusion(f32[256,1024]{1,0:T(8,128)S(1)} %copy-done, f32[256]{0:T(256)S(1)} %copy-done.5, f32[8,64]{1,0:T(8,128)S(1)} %rsqrt.28, f32[8,64]{1,0:T(8,128)S(1)} %div.42, f32[8,8,8,256]{3,2,1,0:T(8,128)} %all-to-all-done), kind=kOutput, calls=%fused_computation.14 | convolution fusion | flops 1611005952 | bytes 3675136 | tf_op jit(solution)/shard_map/vmap()/dot_general | solution.py:26
  102.1 1.2 fusion.43
  103.3 2.4 %copy.53 = f32[8,64,256]{1,2,0:T(8,128)} copy(f32[8,64,256]{2,1,0:T(8,128)} %get-tuple-element.3) | data formatting | bytes 1048576 | tf_op jit(solution)/shard_map/vmap()/mul | solution.py:29
  105.7 2.4 %copy.54 = f32[8,64,256]{1,2,0:T(8,128)} copy(f32[8,64,256]{2,1,0:T(8,128)} %get-tuple-element.2) | data formatting | bytes 1048576 | tf_op jit(solution)/shard_map/vmap()/slice | solution.py:32
  108.1 2.4 %copy.52 = f32[8,64,256]{1,2,0:T(8,128)} copy(f32[8,64,256]{2,1,0:T(8,128)} %get-tuple-element.4) | data formatting | bytes 1048576 | tf_op jit(solution)/shard_map/vmap()/slice | solution.py:33
  110.5 5.1 %add_reduce_fusion = (f32[8,8,64]{2,1,0:T(8,128)S(1)}, f32[8,8,64,64]{2,3,1,0:T(8,128)S(1)}) fusion(f32[8,64,64]{1,2,0:T(8,128)S(1)} %copy.62, f32[8,64,8,32]{1,3,2,0:T(8,128)} %bitcast.83, f32[8,64,8,32]{1,3,2,0:T(8,128)} %bitcast.84), kind=kOutput, calls=%fused_computation.5 | convolution fusion | flops 101183488 | bytes 2244608 | tf_op jit(solution)/shard_map/vmap(ihd,jhd->hij)/dot_general | solution.py:35
  116.8 3.3 %fusion.1 = f32[8,8,32,64]{3,2,1,0:T(8,128)} fusion(f32[8,64,8,32]{1,3,2,0:T(8,128)S(1)} %bitcast.88, f32[8,8,64,64]{2,3,1,0:T(8,128)S(1)} %get-tuple-element.10, f32[8,8,64]{2,1,0:T(8,128)S(1)} %fusion.3, f32[8,8,64]{2,1,0:T(8,128)S(1)} %get-tuple-element.9, f32[8,64,64]{1,2,0:T(8,128)S(1)} %copy.62), kind=kOutput, calls=%fused_computation.2 | convolution fusion | flops 101449728 | bytes 2260992 | tf_op jit(solution)/shard_map/vmap(hij,jhd->ihd)/dot_general | solution.py:37
  120.2 2.3 %copy.64 = f32[8,64,256]{2,1,0:T(8,128)} copy(f32[8,64,256]{1,2,0:T(8,128)} %bitcast.89) | data formatting | bytes 1048576 | tf_op jit(solution)/shard_map/vmap()/reshape | solution.py:37
  122.5 2.0 %fusion.4 = f32[1,8,64,256]{3,2,1,0:T(8,128)S(1)} fusion(f32[8,64,256]{2,1,0:T(8,128)} %copy.64, f32[8,64,1024]{2,1,0:T(8,128)S(1)} %fusion.7, f32[256,256]{1,0:T(8,128)} %param.19, f32[8,8,8,256]{3,2,1,0:T(8,128)} %all-to-all-done), kind=kOutput, calls=%fused_computation.8 | convolution fusion | flops 403308544 | bytes 2359296 | tf_op jit(solution)/shard_map/vmap()/dot_general | solution.py:41
  124.8 19.8 %all_to_all.50 = f32[1,8,64,256]{3,1,0,2:T(8,128)S(1)} all-to-all(f32[1,8,64,256]{3,1,0,2:T(8,128)S(1)} %copy.65), channel_id=1, replica_groups=mesh['seq'=4,'res'=8] {'res'}, dimensions={2} | all-to-all | bytes 1048576 | tf_op jit(solution)/shard_map/all_to_all | solution.py:94
  (40 shorter events, 5.7 us)
Async XLA Ops:
  0.6 98.5 %copy-start = (f32[256,1024]{1,0:T(8,128)S(1)}, f32[256,1024]{1,0:T(8,128)}, u32[]{:S(2)}) copy-start(f32[256,1024]{1,0:T(8,128)} %param.18) | copy-start | bytes 3145732
  7.0 33.9 %all-to-all-start.1 = ((f32[4,1,16384]{2,1,0:T(1,128)}), f32[4,1,16384]{2,1,0:T(1,128)S(1)}, u32[]{:S(2)}, u32[]{:S(2)}) async-start(f32[4,1,16384]{2,1,0:T(1,128)} %reshape.104), calls=%async_computation.1 | async-start | bytes 524288 | tf_op jit(solution)/shard_map/all_to_all | solution.py:11
  40.8 12.7 %all-to-all-start.2 = ((f32[4,1,32768]{2,1,0:T(1,128)}), f32[4,1,32768]{2,1,0:T(1,128)S(1)}, u32[]{:S(2)}, u32[]{:S(2)}) async-start(f32[4,1,32768]{2,1,0:T(1,128)} %reshape.102), calls=%async_computation.2 | async-start | bytes 1048576 | tf_op jit(solution)/shard_map/all_to_all | solution.py:69
  53.5 42.9 %all-to-all-start = ((f32[8,8,8,256]{3,2,1,0:T(8,128)}), f32[8,8,8,256]{3,2,1,0:T(8,128)}, u32[]{:S(2)}, u32[]{:S(2)}) async-start(f32[8,8,8,256]{3,2,1,0:T(8,128)} %bitcast), calls=%async_computation | async-start | bytes 1048576 | tf_op jit(solution)/shard_map/all_to_all | solution.py:87
  68.2 2.5 %copy-start.2 = (f32[1024,128]{1,0:T(8,128)S(1)}, f32[1024,128]{1,0:T(8,128)}, u32[]{:S(2)}) copy-start(f32[1024,128]{1,0:T(8,128)} %param.14) | copy-start | bytes 1572868
  68.3 2.5 %copy-start.4 = (f32[16,8,128]{2,1,0:T(8,128)S(1)}, f32[16,8,128]{2,1,0:T(8,128)}, u32[]{:S(2)}) copy-start(f32[16,8,128]{2,1,0:T(8,128)} %param.11) | copy-start | bytes 196612
  68.3 3.5 %copy-start.6 = (f32[128,8]{0,1:T(8,128)S(1)}, f32[128,8]{0,1:T(8,128)}, u32[]{:S(2)}) copy-start(f32[128,8]{0,1:T(8,128)} %param.16) | copy-start | bytes 12292
  68.3 3.5 %copy-start.7 = (f32[128]{0:T(128)S(1)}, f32[128]{0:T(128)}, u32[]{:S(2)}) copy-start(f32[128]{0:T(128)} %param.15) | copy-start | bytes 1540
  71.5 30.6 %copy-start.3 = (f32[16,8,128]{2,1,0:T(8,128)}, f32[16,8,128]{2,1,0:T(8,128)S(1)}, u32[]{:S(2)}) copy-start(f32[16,8,128]{2,1,0:T(8,128)S(1)} %get-tuple-element.8) | copy-start | bytes 196612
  71.5 27.7 %copy-start.5 = (f32[256]{0:T(256)S(1)}, f32[256]{0:T(256)}, u32[]{:S(2)}) copy-start(f32[256]{0:T(256)} %param.17) | copy-start | bytes 3076
  115.6 1.2 copy-start.1
